TPU v7x, 32 devices: a whole 2x2x4 slice. The times are simulated.
32 devices in a mesh: groups: 2 (over y), wide: 4 (over z), narrow: 4 (over x, core).
Axes of the slice: x: 2, y: 2, z: 4, core: 2. Of those that a mesh axis runs over, the one named last changes fastest.
Arguments:
- generator: int32 [8192], P('narrow'), may hold values from 1 to 511
- lattice_shift: int32 [16384], P(('groups', 'narrow')), parts along dimension 0, may hold values from 0 to 1023
- loadings: bfloat16 [512, 4, 64, 128], P(('groups', 'wide')), parts along dimension 0, may hold values from -0.375 to 0.375
- load_pattern: int32 [512, 4], P(('groups', 'wide')), parts along dimension 0, may hold values from 0 to 127
- threshold: float32 [65536], P(('groups', 'wide')), parts along dimension 0, may hold values from -2.5 to -0.5
- exposure: float32 [65536], P(('groups', 'wide')), parts along dimension 0, may hold values from 0.1 to 2
- segment_map: int32 [65536], P(('groups', 'wide')), parts along dimension 0, may hold values from 0 to 4095, as said below
- net_tiles: bfloat16 [64, 8, 128, 128], P(('groups', 'wide')), parts along dimension 0, may hold values from -0.1875 to 0.1875
- net_pattern: int32 [64, 8], P(('groups', 'wide')), parts along dimension 0, may hold values from 0 to 7
Outputs:
- net_loss: float32 [512, 8192], P('narrow', ('groups', 'wide')), parts along dimension 1
- moments: float32 [2, 8192], P(None, ('groups', 'wide')), parts along dimension 1
There are 2 independent parts, one for each index of `groups`. A program takes and returns all parts, laid end to end along the dimension named above; an argument that names none is the same for every part. Nothing has to cross between parts.
Inputs may be any that keep to these rules, and one draw needn't show every extreme that they name: `segment_map`: in each aligned block of 8192 obligors at most 3072 map to the same group of 1024 consecutive segments; one group receives exactly 3072 obligors from every block.
All inputs are finite; a program needn't handle non-finite values.
Results may differ from a plain program's by a relative error of at most 0.0036.
Values may be sent and summed in bfloat16 or wider, within the bound.
No kernel may reach another device: no remote copies, remote signals or barrier semaphores. Data moves between devices by JAX's collectives and lax.ppermute only.
A program may use at most 64 MiB of HBM per device.

v0:
```python
import jax
import jax.numpy as jnp
from jax import lax
from jax.sharding import PartitionSpec as P

P_SIZE = 512
SEG_DEV = 1024


def normal_cdf(values):
    return 0.5 * lax.erfc(-values * 0.7071067811865476)


def normal_quantile(values):
    return 1.4142135623730951 * lax.erf_inv(2.0 * values - 1.0)


def normal_points(count, generator, lattice_shift):
    points = jnp.arange(count, dtype=jnp.int32)
    residue = points[:, None] * generator[None, :] % P_SIZE
    offset = (lattice_shift.astype(jnp.float32) + 0.5) / 1024.0
    uniform = (residue.astype(jnp.float32) + offset[None, :]) / P_SIZE
    return normal_quantile(uniform).astype(jnp.bfloat16)


def body(
    generator,
    lattice_shift,
    loadings,
    load_pattern,
    threshold,
    exposure,
    segment_map,
    net_tiles,
    net_pattern,
):
    narrow_size = lax.axis_size("narrow")
    local_points = P_SIZE // narrow_size
    panel = normal_points(P_SIZE, generator, lattice_shift)
    factors = lax.all_to_all(panel, "narrow", split_axis=0, concat_axis=1, tiled=True)
    factor_width = factors.shape[1]
    factor_tiles = factors.T.reshape(factor_width // 64, 64, local_points)
    picked = factor_tiles[load_pattern]
    latent = jnp.einsum("bkfp,bkfi->pbi", picked, loadings, preferred_element_type=jnp.float32)
    latent = latent.reshape(local_points, -1)
    default_prob = normal_cdf(threshold[None, :] - latent)
    weighted = (exposure[None, :] * default_prob).astype(jnp.bfloat16)
    by_row = weighted.T
    groups = lax.axis_size("wide")
    partial_sums = jax.ops.segment_sum(
        by_row.astype(jnp.float32), segment_map, num_segments=groups * SEG_DEV
    )
    seg_loss = lax.psum_scatter(partial_sums, "wide", scatter_dimension=0, tiled=True)
    loss_blocks = seg_loss.astype(jnp.bfloat16).reshape(-1, 128, local_points)
    gathered = loss_blocks[net_pattern]
    netted = jnp.einsum("bkjp,bkji->pbi", gathered, net_tiles, preferred_element_type=jnp.float32)
    netted = netted.reshape(local_points, -1)
    first_sum, second_sum = lax.psum(
        (jnp.sum(netted, axis=0), jnp.sum(netted * netted, axis=0)), "narrow"
    )
    moments = jnp.stack([first_sum, second_sum]) / P_SIZE
    return (netted, moments)


def solution(mesh):
    return jax.shard_map(
        body,
        mesh=mesh,
        in_specs=(
            P("narrow"),
            P(("groups", "narrow")),
            P(("groups", "wide"), None, None, None),
            P(("groups", "wide"), None),
            P(("groups", "wide")),
            P(("groups", "wide")),
            P(("groups", "wide")),
            P(("groups", "wide"), None, None, None),
            P(("groups", "wide"), None),
        ),
        out_specs=(P("narrow", ("groups", "wide")), P(None, ("groups", "wide"))),
        check_vma=False,
    )
```

profile of v0, /device:TPU:0, one launch (start us, length us, event | category | flops | bytes accessed | tf_op | source)
XLA Modules:
  0.0 184.4 jit_solution(4201307887410369890)
XLA Ops:
  7.2 0.0 copy-start
  7.2 0.0 copy-start.4
  7.2 0.0 copy-start.2
  7.2 0.8 add_multiply_fusion
  8.1 12.4 %multiply_convert_fusion = bf16[4,128,2048]{1,2,0:T(8,128)(2,1)} fusion(f32[2048]{0:T(1024)S(1)} %add_multiply_fusion, s32[2048]{0:T(1024)} %param.9, s32[4,128]{1,0:T(4,128)S(1)} %multiply_add_fusion), kind=kLoop, calls=%fused_computation.38 | loop fusion | flops 57671680 | bytes 2115584 | tf_op jit(solution)/shard_map/convert_element_type | solution.py:23
  20.4 4.4 %all-to-all-start = ((bf16[4,128,2048]{1,2,0:T(8,128)(2,1)}), bf16[4,128,2048]{1,2,0:T(8,128)(2,1)}, u32[]{:S(2)}, u32[]{:S(2)}) async-start(bf16[4,128,2048]{1,2,0:T(8,128)(2,1)} %multiply_convert_fusion), calls=%async_computation | async-start | bytes 4194304 | tf_op jit(solution)/shard_map/all_to_all | solution.py:40
  24.9 0.0 reduce-scatter.2.cloned.1.call-start
  24.9 0.0 copy-done.4
  25.0 0.1 copy.13
  25.1 0.1 reshape.52
  25.2 0.0 copy-done.2
  25.2 26.1 %all-to-all-done = bf16[4,128,2048]{1,2,0:T(8,128)(2,1)} async-done(((bf16[4,128,2048]{1,2,0:T(8,128)(2,1)}), bf16[4,128,2048]{1,2,0:T(8,128)(2,1)}, u32[]{:S(2)}, u32[]{:S(2)}) %all-to-all-start) | async-done | bytes 2097184 | tf_op jit(solution)/shard_map/all_to_all | solution.py:40
  51.3 4.6 %gather_fusion = bf16[256,64,128]{2,1,0:T(8,128)(2,1)} fusion(bf16[128,64,128]{2,1,0:T(8,128)(2,1)} %bitcast.3, s32[1024]{0:T(1024)S(1)} %pad_clamp_fusion.1), kind=kCustom, calls=%fused_computation | custom fusion | bytes 8389632 | tf_op jit(solution)/shard_map/gather | solution.py:43
  55.9 0.0 copy-start.1
  55.9 4.8 %fusion.24 = f32[64,128,128,1]{1,2,3,0:T(8,128)S(1)} fusion(bf16[64,4,64,128]{3,2,1,0:T(8,128)(2,1)} %bitcast.43, bf16[64,4,64,128]{3,2,1,0:T(8,128)(2,1)} %param.11), kind=kOutput, calls=%fused_computation.54 | convolution fusion | flops 536870912 | bytes 12582912 | tf_op jit(solution)/shard_map/bkfp,bkfi->pbi/dot_general | solution.py:44
  60.7 0.0 copy-done.1
  60.7 11.9 %fusion.8 = bf16[128,8192]{0,1:T(8,128)(2,1)} fusion(f32[64,128,128,1]{1,2,3,0:T(8,128)S(1)} %fusion.24, f32[8192]{0:T(1024)S(1)} %broadcast_multiply_fusion, f32[8192]{0:T(1024)S(1)} %copy-done.1), kind=kLoop, calls=%fused_computation.18 | loop fusion | flops 68157440 | bytes 6356992 | tf_op jit(solution)/shard_map/convert_element_type | solution.py:47
  72.6 0.0 copy-start.3
  72.6 46.0 %scatter_custom_fusion = f32[4096,128]{1,0:T(8,128)} fusion(s32[8192]{0:T(1024)} %param.15, bf16[128,8192]{0,1:T(8,128)(2,1)} %fusion.8, f32[]{:T(128)} %constant.62.clone.1), kind=kCustom, calls=%fused_computation.23 | custom fusion | flops 2097152 | bytes 4194816 | tf_op jit(solution)/shard_map/scatter-add | solution.py:50
  118.5 0.0 reduce-scatter.2.cloned.1.call-update
  118.6 0.0 copy-done.3
  118.6 0.1 reshape.60
  118.7 45.0 %reduce-scatter.2.cloned.1.call-done = f32[1024,128]{1,0:T(8,128)} async-done(((f32[4096,128]{1,0:T(8,128)}), f32[1024,128]{1,0:T(8,128)}) %reduce-scatter.2.cloned.1.call-update) | async-done | bytes 524304 | tf_op jit(solution)/shard_map/reduce_scatter | solution.py:53
  163.7 1.1 convert_element_type.29
  164.8 2.2 %gather_fusion.1 = bf16[64,128,128]{2,1,0:T(8,128)(2,1)} fusion(bf16[8,128,128]{2,1,0:T(8,128)(2,1)S(1)} %bitcast.42, s32[1024]{0:T(1024)S(1)} %pad_clamp_fusion), kind=kCustom, calls=%fused_computation.1 | custom fusion | bytes 4194560 | tf_op jit(solution)/shard_map/gather | solution.py:55
  167.0 0.0 copy-done
  167.0 2.5 %bitcast_reduce_fusion = (f32[8,128]{1,0:T(8,128)S(1)}, f32[8,128]{1,0:T(8,128)S(1)}, f32[8,128,128,1]{1,2,3,0:T(8,128)S(1)}) fusion(bf16[8,8,128,128]{3,2,1,0:T(8,128)(2,1)} %bitcast.44, bf16[8,8,128,128]{3,2,1,0:T(8,128)(2,1)S(1)} %copy-done), kind=kOutput, calls=%fused_computation.43 | convolution fusion | flops 268826624 | bytes 4726784 | tf_op jit(solution)/shard_map/bkjp,bkji->pbi/dot_general | solution.py:56
  169.5 1.0 copy.15
  170.5 6.5 %all-reduce = (f32[1,1024]{1,0:T(1,128)S(1)}, f32[1,1024]{1,0:T(1,128)S(1)}) all-reduce(f32[1,1024]{1,0:T(1,128)S(1)} %bitcast.47, f32[1,1024]{1,0:T(1,128)S(1)} %bitcast.46), channel_id=1, replica_groups=mesh['groups'=2,'wide'=4,'narrow'=4] {'narrow'}, use_global_device_ids=true, to_apply=%region_5.6 | all-reduce | flops 2048 | bytes 16384 | tf_op jit(solution)/shard_map/psum | solution.py:58
  177.0 0.6 maximum_multiply_fusion
  (6 shorter events, 0.0 us)
Async XLA Ops:
  7.2 159.8 %copy-start = (bf16[8,8,128,128]{3,2,1,0:T(8,128)(2,1)S(1)}, bf16[8,8,128,128]{3,2,1,0:T(8,128)(2,1)}, u32[]{:S(2)}) copy-start(bf16[8,8,128,128]{3,2,1,0:T(8,128)(2,1)} %param.16) | copy-start | bytes 6291460
  7.2 17.8 %copy-start.4 = (s32[64,4]{0,1:T(4,128)S(1)}, s32[64,4]{0,1:T(4,128)}, u32[]{:S(2)}) copy-start(s32[64,4]{0,1:T(4,128)} %param.12) | copy-start | bytes 3076
  7.2 18.0 %copy-start.2 = (f32[8192]{0:T(1024)S(1)}, f32[8192]{0:T(1024)}, u32[]{:S(2)}) copy-start(f32[8192]{0:T(1024)} %param.14) | copy-start | bytes 98308
  20.4 30.8 %all-to-all-start = ((bf16[4,128,2048]{1,2,0:T(8,128)(2,1)}), bf16[4,128,2048]{1,2,0:T(8,128)(2,1)}, u32[]{:S(2)}, u32[]{:S(2)}) async-start(bf16[4,128,2048]{1,2,0:T(8,128)(2,1)} %multiply_convert_fusion), calls=%async_computation | async-start | bytes 4194304 | tf_op jit(solution)/shard_map/all_to_all | solution.py:40
  24.9 138.8 %reduce-scatter.2.cloned.1.call-start = ((), (), s32[]{:S(2)}) async-start(), calls=%async_computation.2 | async-start | bytes 2621440 | tf_op jit(solution)/shard_map/reduce_scatter | solution.py:53
  55.9 4.8 %copy-start.1 = (f32[8192]{0:T(1024)S(1)}, f32[8192]{0:T(1024)}, u32[]{:S(2)}) copy-start(f32[8192]{0:T(1024)} %param.13) | copy-start | bytes 98308
  72.6 46.0 %copy-start.3 = (s32[8,8]{1,0:T(8,128)S(1)}, s32[8,8]{1,0:T(8,128)}, u32[]{:S(2)}) copy-start(s32[8,8]{1,0:T(8,128)} %param.17) | copy-start | bytes 772
Sparse Core Ops, SparseCore 0:
  118.7 44.9 reduce-scatter.1
where the time goes:
time: 185 us; the launch traced here: 184 us
  other arithmetic  72.8 us (39%)
  waiting for transfers between devices  71.1 us (38%)
  between operations  14.2 us (8%)
  local copies, waits for them, and re-layouts  8.08 us (4%)
  matrix products  7.29 us (4%)
  blocking collectives  6.49 us (4%)
  starting transfers between devices  4.48 us (2%)
    scatter-add x1, other arithmetic, body(): jax.ops.segment_sum(by_row.astype(jnp.float32), segment_map, num_segments...  46 us
    reduce_scatter x1, waiting for transfers between devices, body(): lax.psum_scatter(partial_sums, 'wide', scatter_dimension=0, tiled=True)  45 us
    all_to_all x1, waiting for transfers between devices, body(): lax.all_to_all(panel, 'narrow', split_axis=0, concat_axis=1, tiled=True)  26.1 us
    convert_element_type x1, other arithmetic, normal_points(): return normal_quantile(uniform).astype(jnp.bfloat16)  12.4 us
    convert_element_type x1, other arithmetic, body(): weighted = (exposure[None, :] * default_prob).astype(jnp.bfloat16)  11.9 us
    psum x1, blocking collectives, body(): lax.psum((jnp.sum(netted, axis=0), jnp.sum(netted * netted, axis=0)), 'na...  6.49 us
    dot_general x1, matrix products, body(): jnp.einsum('bkfp,bkfi->pbi', picked, loadings, preferred_element_type=jnp...  4.77 us
    gather x1, local copies, waits for them, and re-layouts, body(): picked = factor_tiles[load_pattern]  4.61 us
  transfers between devices with their start and end apart: 2, of which 2 were waited for; matrix products, arithmetic and copies ran while one was open for 0% of the time, Pallas kernels for 0%

commit v1 on v0

--- a/solution.py
+++ b/solution.py
@@ -37,7 +37,12 @@
     narrow_size = lax.axis_size("narrow")
     local_points = P_SIZE // narrow_size
     panel = normal_points(P_SIZE, generator, lattice_shift)
-    factors = lax.all_to_all(panel, "narrow", split_axis=0, concat_axis=1, tiled=True)
+    factors = jnp.concatenate(
+        lax.all_to_all(
+            jnp.stack(jnp.split(panel, lax.axis_size("narrow"), axis=0)), "narrow", 0, 0
+        ),
+        axis=1,
+    )
     factor_width = factors.shape[1]
     factor_tiles = factors.T.reshape(factor_width // 64, 64, local_points)
     picked = factor_tiles[load_pattern]

time: 185 us -> 186 us (level)
  no operation moved by 1% of the time
where the time goes in v1:
time: 186 us
  other arithmetic  73.6 us (40%)
  waiting for transfers between devices  71.2 us (38%)
  between operations  14.2 us (8%)
  local copies, waits for them, and re-layouts  8.45 us (5%)
  matrix products  7.28 us (4%)
  blocking collectives  6.47 us (3%)
  starting transfers between devices  4.48 us (2%)
    scatter-add x1, other arithmetic, body(): jax.ops.segment_sum(by_row.astype(jnp.float32), segment_map, num_segments...  46 us
    reduce_scatter x1, waiting for transfers between devices, body(): lax.psum_scatter(partial_sums, 'wide', scatter_dimension=0, tiled=True)  45.1 us
    all_to_all x1, waiting for transfers between devices, body(): lax.all_to_all(jnp.stack(jnp.split(panel, lax.axis_size('narrow'), axis=0...  26.1 us
    convert_element_type x1, other arithmetic, body(): weighted = (exposure[None, :] * default_prob).astype(jnp.bfloat16)  11.9 us
    convert_element_type x1, other arithmetic, normal_points(): return normal_quantile(uniform).astype(jnp.bfloat16)  11.6 us
    psum x1, blocking collectives, body(): lax.psum((jnp.sum(netted, axis=0), jnp.sum(netted * netted, axis=0)), 'na...  6.47 us
    dot_general x1, matrix products, body(): jnp.einsum('bkfp,bkfi->pbi', picked, loadings, preferred_element_type=jnp...  4.76 us
    gather x1, local copies, waits for them, and re-layouts, body(): picked = factor_tiles[load_pattern]  4.61 us
  transfers between devices with their start and end apart: 2, of which 2 were waited for; matrix products, arithmetic and copies ran while one was open for 0% of the time, Pallas kernels for 0%

profile of v1, /device:TPU:0, one launch (start us, length us, event | category | flops | bytes accessed | tf_op | source)
XLA Modules:
  0.0 185.7 jit_solution(17928653216072321599)
XLA Ops:
  7.2 0.0 copy-start
  7.2 0.8 add_multiply_fusion
  8.0 11.6 %multiply_convert_fusion = bf16[512,2048]{0,1:T(8,128)(2,1)S(1)} fusion(f32[2048]{0:T(1024)S(1)} %add_multiply_fusion, s32[2048]{0:T(1024)} %param.9), kind=kLoop, calls=%fused_computation.36 | loop fusion | flops 57671680 | bytes 2113536 | tf_op jit(solution)/shard_map/convert_element_type | solution.py:23
  19.6 0.4 slice_bitcast_fusion.3
  20.0 0.0 copy-start.4
  20.0 0.0 copy-start.2
  20.0 1.6 pad_maximum_fusion
  21.6 4.4 %all-to-all-start = ((bf16[4,128,2048]{1,2,0:T(8,128)(2,1)}), bf16[4,128,2048]{1,2,0:T(8,128)(2,1)}, u32[]{:S(2)}, u32[]{:S(2)}) async-start(bf16[4,128,2048]{1,2,0:T(8,128)(2,1)} %pad_maximum_fusion), calls=%async_computation | async-start | bytes 4194304 | tf_op jit(solution)/shard_map/all_to_all | solution.py:41
  26.1 0.0 reduce-scatter.2.cloned.1.call-start
  26.1 0.0 copy-done.4
  26.2 0.1 copy.13
  26.3 0.1 reshape.38
  26.4 0.0 copy-done.2
  26.4 26.1 %all-to-all-done = bf16[4,128,2048]{1,2,0:T(8,128)(2,1)} async-done(((bf16[4,128,2048]{1,2,0:T(8,128)(2,1)}), bf16[4,128,2048]{1,2,0:T(8,128)(2,1)}, u32[]{:S(2)}, u32[]{:S(2)}) %all-to-all-start) | async-done | bytes 2097184 | tf_op jit(solution)/shard_map/all_to_all | solution.py:41
  52.5 4.6 %gather_fusion = bf16[256,64,128]{2,1,0:T(8,128)(2,1)} fusion(bf16[128,64,128]{2,1,0:T(8,128)(2,1)} %bitcast.7, s32[1024]{0:T(1024)S(1)} %pad_clamp_fusion.1), kind=kCustom, calls=%fused_computation | custom fusion | bytes 8389632 | tf_op jit(solution)/shard_map/gather | solution.py:48
  57.1 0.0 copy-start.1
  57.1 4.8 %fusion.27 = f32[64,128,128,1]{1,2,3,0:T(8,128)S(1)} fusion(bf16[64,4,64,128]{3,2,1,0:T(8,128)(2,1)} %bitcast.51, bf16[64,4,64,128]{3,2,1,0:T(8,128)(2,1)} %param.11), kind=kOutput, calls=%fused_computation.59 | convolution fusion | flops 536870912 | bytes 12582912 | tf_op jit(solution)/shard_map/bkfp,bkfi->pbi/dot_general | solution.py:49
  61.9 0.0 copy-done.1
  61.9 11.9 %fusion.9 = bf16[128,8192]{0,1:T(8,128)(2,1)} fusion(f32[64,128,128,1]{1,2,3,0:T(8,128)S(1)} %fusion.27, f32[8192]{0:T(1024)S(1)} %broadcast_multiply_fusion, f32[8192]{0:T(1024)S(1)} %copy-done.1), kind=kLoop, calls=%fused_computation.17 | loop fusion | flops 68157440 | bytes 6356992 | tf_op jit(solution)/shard_map/convert_element_type | solution.py:52
  73.8 0.0 copy-start.3
  73.8 46.0 %scatter_custom_fusion = f32[4096,128]{1,0:T(8,128)} fusion(s32[8192]{0:T(1024)} %param.15, bf16[128,8192]{0,1:T(8,128)(2,1)} %fusion.9, f32[]{:T(128)} %constant.62.clone.1), kind=kCustom, calls=%fused_computation.21 | custom fusion | flops 2097152 | bytes 4194816 | tf_op jit(solution)/shard_map/scatter-add | solution.py:55
  119.8 0.0 reduce-scatter.2.cloned.1.call-update
  119.8 0.0 copy-done.3
  119.8 0.1 reshape.46
  119.9 45.1 %reduce-scatter.2.cloned.1.call-done = f32[1024,128]{1,0:T(8,128)} async-done(((f32[4096,128]{1,0:T(8,128)}), f32[1024,128]{1,0:T(8,128)}) %reduce-scatter.2.cloned.1.call-update) | async-done | bytes 524304 | tf_op jit(solution)/shard_map/reduce_scatter | solution.py:58
  165.0 1.1 convert_element_type.27
  166.0 2.2 %gather_fusion.1 = bf16[64,128,128]{2,1,0:T(8,128)(2,1)} fusion(bf16[8,128,128]{2,1,0:T(8,128)(2,1)S(1)} %bitcast.50, s32[1024]{0:T(1024)S(1)} %pad_clamp_fusion), kind=kCustom, calls=%fused_computation.1 | custom fusion | bytes 4194560 | tf_op jit(solution)/shard_map/gather | solution.py:60
  168.2 0.0 copy-done
  168.2 2.5 %bitcast_reduce_fusion = (f32[8,128]{1,0:T(8,128)S(1)}, f32[8,128]{1,0:T(8,128)S(1)}, f32[8,128,128,1]{1,2,3,0:T(8,128)S(1)}) fusion(bf16[8,8,128,128]{3,2,1,0:T(8,128)(2,1)} %bitcast.52, bf16[8,8,128,128]{3,2,1,0:T(8,128)(2,1)S(1)} %copy-done), kind=kOutput, calls=%fused_computation.49 | convolution fusion | flops 268826624 | bytes 4726784 | tf_op jit(solution)/shard_map/bkjp,bkji->pbi/dot_general | solution.py:61
  170.7 1.0 copy.15
  171.7 6.5 %all-reduce = (f32[1,1024]{1,0:T(1,128)S(1)}, f32[1,1024]{1,0:T(1,128)S(1)}) all-reduce(f32[1,1024]{1,0:T(1,128)S(1)} %bitcast.55, f32[1,1024]{1,0:T(1,128)S(1)} %bitcast.54), channel_id=1, replica_groups=mesh['groups'=2,'wide'=4,'narrow'=4] {'narrow'}, use_global_device_ids=true, to_apply=%region_5.6 | all-reduce | flops 2048 | bytes 16384 | tf_op jit(solution)/shard_map/psum | solution.py:63
  178.2 0.6 maximum_multiply_fusion
  (5 shorter events, 0.0 us)
Async XLA Ops:
  7.2 161.0 %copy-start = (bf16[8,8,128,128]{3,2,1,0:T(8,128)(2,1)S(1)}, bf16[8,8,128,128]{3,2,1,0:T(8,128)(2,1)}, u32[]{:S(2)}) copy-start(bf16[8,8,128,128]{3,2,1,0:T(8,128)(2,1)} %param.16) | copy-start | bytes 6291460
  20.0 6.1 %copy-start.4 = (s32[64,4]{0,1:T(4,128)S(1)}, s32[64,4]{0,1:T(4,128)}, u32[]{:S(2)}) copy-start(s32[64,4]{0,1:T(4,128)} %param.12) | copy-start | bytes 3076
  20.0 6.4 %copy-start.2 = (f32[8192]{0:T(1024)S(1)}, f32[8192]{0:T(1024)}, u32[]{:S(2)}) copy-start(f32[8192]{0:T(1024)} %param.14) | copy-start | bytes 98308
  21.6 30.8 %all-to-all-start = ((bf16[4,128,2048]{1,2,0:T(8,128)(2,1)}), bf16[4,128,2048]{1,2,0:T(8,128)(2,1)}, u32[]{:S(2)}, u32[]{:S(2)}) async-start(bf16[4,128,2048]{1,2,0:T(8,128)(2,1)} %pad_maximum_fusion), calls=%async_computation | async-start | bytes 4194304 | tf_op jit(solution)/shard_map/all_to_all | solution.py:41
  26.1 138.9 %reduce-scatter.2.cloned.1.call-start = ((), (), s32[]{:S(2)}) async-start(), calls=%async_computation.2 | async-start | bytes 2621440 | tf_op jit(solution)/shard_map/reduce_scatter | solution.py:58
  57.1 4.8 %copy-start.1 = (f32[8192]{0:T(1024)S(1)}, f32[8192]{0:T(1024)}, u32[]{:S(2)}) copy-start(f32[8192]{0:T(1024)} %param.13) | copy-start | bytes 98308
  73.8 46.0 %copy-start.3 = (s32[8,8]{1,0:T(8,128)S(1)}, s32[8,8]{1,0:T(8,128)}, u32[]{:S(2)}) copy-start(s32[8,8]{1,0:T(8,128)} %param.17) | copy-start | bytes 772
Sparse Core Ops, SparseCore 0:
  119.9 45.0 reduce-scatter.1
